TPU v7x, 512 devices: a whole 4x8x8 slice. The times are simulated.
512 devices in a mesh: gx: 32 (over z, x), gy: 16 (over y, core).
Axes of the slice: x: 4, y: 8, z: 8, core: 2. Of those that a mesh axis runs over, the one named last changes fastest.
Arguments:
- source: float32 [2048, 256, 128], P('gx', 'gy'), may hold values from -5 to 5
Outputs:
- pressure: float32 [2048, 256, 128], P('gx', 'gy')
All inputs are finite; a program needn't handle non-finite values.
Results may differ from a plain program's by a relative error of at most 0.0003.
Values sent between devices are 32-bit elements; how exact they have to be, the bound alone decides.
A program may use at most 64 MiB of HBM per device.

v0:
```python
import math
import jax
import jax.numpy as jnp
from jax import lax
from jax.sharding import PartitionSpec as P

SCREEN = 32
highest = lax.Precision.HIGHEST


def cosine_table(points, wavenums, places):
    angles = wavenums[:, None] * (2 * places[None, :] + 1) % (4 * points)
    norming = jnp.where(wavenums == 0, math.sqrt(1.0 / points), math.sqrt(2.0 / points)).astype(
        jnp.float32
    )
    return norming[:, None] * jnp.cos(angles.astype(jnp.float32) * (math.pi / (2 * points)))


def eigenvalue(wavenums, points):
    half_angle = jnp.sin(wavenums.astype(jnp.float32) * (math.pi / (2 * points)))
    return 4.0 * half_angle * half_angle


def forward_cosine(received):
    length = received.shape[2]
    width = min(256, length)
    places = jnp.arange(length, dtype=jnp.int32)

    def forward_one_block(index, output):
        offset = index * width
        cos_table = cosine_table(length, offset + jnp.arange(width, dtype=jnp.int32), places)
        piece = jnp.einsum("zyx,kx->zyk", received, cos_table, precision=highest)
        return lax.dynamic_update_slice_in_dim(output, piece, offset, 2)

    return lax.fori_loop(
        0, length // width, forward_one_block, jnp.zeros(received.shape, jnp.float32)
    )


def backward_cosine(solved):
    length = solved.shape[2]
    width = min(256, length)
    waves = jnp.arange(length, dtype=jnp.int32)

    def backward_one_block(index, output):
        offset = index * width
        cos_table = cosine_table(length, waves, offset + jnp.arange(width, dtype=jnp.int32))
        piece = jnp.einsum("zyk,kx->zyx", solved, cos_table, precision=highest)
        return lax.dynamic_update_slice_in_dim(output, piece, offset, 2)

    return lax.fori_loop(
        0, length // width, backward_one_block, jnp.zeros(solved.shape, jnp.float32)
    )


def thomas(rhs_lines, diagonal):

    def forward_step(carry, source_line):
        factor, eliminated = carry
        factor = 1.0 / (diagonal - factor)
        eliminated = (source_line + eliminated) * factor
        return ((factor, eliminated), (factor, eliminated))

    empty_line = jnp.zeros_like(rhs_lines[0])
    unused, (factors, eliminated) = lax.scan(
        forward_step, (empty_line, empty_line), rhs_lines, unroll=8
    )

    def backward_step(pressure_next, inputs_line):
        solved_line = inputs_line[1] + inputs_line[0] * pressure_next
        return (solved_line, solved_line)

    unused_last, solution = lax.scan(
        backward_step, empty_line, (factors, eliminated), reverse=True, unroll=8
    )
    return solution


def shards(source):
    cx_cells, cy_cells, nz_cells = source.shape
    planes = nz_cells // lax.axis_size("gx")
    plane_first = lax.axis_index("gx") * planes
    nz_waves = jnp.arange(nz_cells, dtype=jnp.int32)
    z_table = cosine_table(nz_cells, nz_waves, nz_waves)
    zhat = jnp.einsum("xyz,kz->kyx", source, z_table, precision=highest)
    spectral = forward_cosine(lax.all_to_all(zhat, "gx", split_axis=0, concat_axis=2, tiled=True))
    nx_cells = spectral.shape[2]
    screen_shift = 1.0 / (SCREEN * SCREEN)
    z_eigen = eigenvalue(plane_first + jnp.arange(planes, dtype=jnp.int32), nz_cells)
    columns = lax.all_to_all(spectral, "gy", split_axis=2, concat_axis=1, tiled=True)
    column_count = columns.shape[2]
    column_first = lax.axis_index("gy") * column_count
    x_eigen = eigenvalue(column_first + jnp.arange(column_count, dtype=jnp.int32), nx_cells)
    diagonal = 2.0 + (screen_shift + z_eigen[:, None] + x_eigen[None, :])
    solved_columns = thomas(jnp.moveaxis(columns, 1, 0), diagonal)
    solved = lax.all_to_all(
        jnp.moveaxis(solved_columns, 0, 1), "gy", split_axis=1, concat_axis=2, tiled=True
    )
    physical = backward_cosine(solved)
    regrouped = lax.all_to_all(physical, "gx", split_axis=2, concat_axis=0, tiled=True)
    return jnp.einsum("kyx,kz->xyz", regrouped, z_table, precision=highest)


def solution(mesh):
    return jax.shard_map(
        shards,
        mesh=mesh,
        in_specs=(P("gx", "gy", None),),
        out_specs=P("gx", "gy", None),
        check_vma=False,
    )
```

profile of v0, /device:TPU:1, one launch (start us, length us, event | category | flops | bytes accessed | tf_op | source)
XLA Modules:
  0.0 354.0 jit_solution(14505402717037691400)
XLA Ops:
  3.9 13.7 %all-to-all-start = ((f32[32,1,4096]{2,1,0:T(1,128)}), f32[32,1,4096]{2,1,0:T(1,128)S(1)}, u32[]{:S(2)}, u32[]{:S(2)}) async-start(f32[32,1,4096]{2,1,0:T(1,128)} %reshape.126), calls=%async_computation | async-start | bytes 1048576 | tf_op jit(solution)/shard_map/all_to_all | solution.py:86
  17.6 16.3 %all-to-all-done = f32[32,1,4096]{2,1,0:T(1,128)S(1)} async-done(((f32[32,1,4096]{2,1,0:T(1,128)}), f32[32,1,4096]{2,1,0:T(1,128)S(1)}, u32[]{:S(2)}, u32[]{:S(2)}) %all-to-all-start) | async-done | bytes 524320 | tf_op jit(solution)/shard_map/all_to_all | solution.py:86
  37.8 77.5 %while.67 = (s32[]{:T(128)}, f32[4,16,2048]{2,1,0:T(8,128)S(1)}, f32[4,16,2048]{2,1,0:T(8,128)S(1)}, s32[]{:T(128)}, s32[]{:T(128)}, /*index=5*/s32[]{:T(128)}, s32[]{:T(128)}) while((s32[]{:T(128)}, f32[4,16,2048]{2,1,0:T(8,128)S(1)}, f32[4,16,2048]{2,1,0:T(8,128)S(1)}, s32[]{:T(128)}, s32[]{:T(128)}, /*index=5*/s32[]{:T(128)}, ...), condition=%wide.region_1.2_spmd.clone, body=%wide.region_0.1_spmd.clone.sunk | while | flops 410522624 | bytes 610439 | solution.py:35
  38.2 9.6 %fusion.161 = f32[4,16,2048]{2,1,0:T(8,128)S(1)} fusion(f32[4,16,2048]{2,1,0:T(8,128)S(1)} %get-tuple-element.753, s32[]{:T(128)S(6)} %select_n.174, f32[4,16,2048]{2,1,0:T(8,128)S(1)} %get-tuple-element.761, s32[2048]{0:T(1024)S(1)} %fusion.160, s32[256]{0:T(256)S(1)} %iota_add_fusion.2, f32[256]{0:T(256)S(1)} %compare_select_fusion.3), kind=kOutput, calls=%fused_computation.19.clone.1 | convolution fusion | flops 410517504 | bytes 600068 | tf_op jit(solution)/shard_map/while/body/eval_jaxpr/zyx,kx->zyk/dot_general | solution.py:32
  47.9 9.6 %fusion.161 = f32[4,16,2048]{2,1,0:T(8,128)S(1)} fusion(f32[4,16,2048]{2,1,0:T(8,128)S(1)} %get-tuple-element.753, s32[]{:T(128)S(6)} %select_n.174, f32[4,16,2048]{2,1,0:T(8,128)S(1)} %get-tuple-element.761, s32[2048]{0:T(1024)S(1)} %fusion.160, s32[256]{0:T(256)S(1)} %iota_add_fusion.2, f32[256]{0:T(256)S(1)} %compare_select_fusion.3), kind=kOutput, calls=%fused_computation.19.clone.1 | convolution fusion | flops 410517504 | bytes 600068 | tf_op jit(solution)/shard_map/while/body/eval_jaxpr/zyx,kx->zyk/dot_general | solution.py:32
  57.5 9.6 %fusion.161 = f32[4,16,2048]{2,1,0:T(8,128)S(1)} fusion(f32[4,16,2048]{2,1,0:T(8,128)S(1)} %get-tuple-element.753, s32[]{:T(128)S(6)} %select_n.174, f32[4,16,2048]{2,1,0:T(8,128)S(1)} %get-tuple-element.761, s32[2048]{0:T(1024)S(1)} %fusion.160, s32[256]{0:T(256)S(1)} %iota_add_fusion.2, f32[256]{0:T(256)S(1)} %compare_select_fusion.3), kind=kOutput, calls=%fused_computation.19.clone.1 | convolution fusion | flops 410517504 | bytes 600068 | tf_op jit(solution)/shard_map/while/body/eval_jaxpr/zyx,kx->zyk/dot_general | solution.py:32
  67.2 9.6 %fusion.161 = f32[4,16,2048]{2,1,0:T(8,128)S(1)} fusion(f32[4,16,2048]{2,1,0:T(8,128)S(1)} %get-tuple-element.753, s32[]{:T(128)S(6)} %select_n.174, f32[4,16,2048]{2,1,0:T(8,128)S(1)} %get-tuple-element.761, s32[2048]{0:T(1024)S(1)} %fusion.160, s32[256]{0:T(256)S(1)} %iota_add_fusion.2, f32[256]{0:T(256)S(1)} %compare_select_fusion.3), kind=kOutput, calls=%fused_computation.19.clone.1 | convolution fusion | flops 410517504 | bytes 600068 | tf_op jit(solution)/shard_map/while/body/eval_jaxpr/zyx,kx->zyk/dot_general | solution.py:32
  76.8 9.6 %fusion.161 = f32[4,16,2048]{2,1,0:T(8,128)S(1)} fusion(f32[4,16,2048]{2,1,0:T(8,128)S(1)} %get-tuple-element.753, s32[]{:T(128)S(6)} %select_n.174, f32[4,16,2048]{2,1,0:T(8,128)S(1)} %get-tuple-element.761, s32[2048]{0:T(1024)S(1)} %fusion.160, s32[256]{0:T(256)S(1)} %iota_add_fusion.2, f32[256]{0:T(256)S(1)} %compare_select_fusion.3), kind=kOutput, calls=%fused_computation.19.clone.1 | convolution fusion | flops 410517504 | bytes 600068 | tf_op jit(solution)/shard_map/while/body/eval_jaxpr/zyx,kx->zyk/dot_general | solution.py:32
  86.5 9.6 %fusion.161 = f32[4,16,2048]{2,1,0:T(8,128)S(1)} fusion(f32[4,16,2048]{2,1,0:T(8,128)S(1)} %get-tuple-element.753, s32[]{:T(128)S(6)} %select_n.174, f32[4,16,2048]{2,1,0:T(8,128)S(1)} %get-tuple-element.761, s32[2048]{0:T(1024)S(1)} %fusion.160, s32[256]{0:T(256)S(1)} %iota_add_fusion.2, f32[256]{0:T(256)S(1)} %compare_select_fusion.3), kind=kOutput, calls=%fused_computation.19.clone.1 | convolution fusion | flops 410517504 | bytes 600068 | tf_op jit(solution)/shard_map/while/body/eval_jaxpr/zyx,kx->zyk/dot_general | solution.py:32
  96.1 9.6 %fusion.161 = f32[4,16,2048]{2,1,0:T(8,128)S(1)} fusion(f32[4,16,2048]{2,1,0:T(8,128)S(1)} %get-tuple-element.753, s32[]{:T(128)S(6)} %select_n.174, f32[4,16,2048]{2,1,0:T(8,128)S(1)} %get-tuple-element.761, s32[2048]{0:T(1024)S(1)} %fusion.160, s32[256]{0:T(256)S(1)} %iota_add_fusion.2, f32[256]{0:T(256)S(1)} %compare_select_fusion.3), kind=kOutput, calls=%fused_computation.19.clone.1 | convolution fusion | flops 410517504 | bytes 600068 | tf_op jit(solution)/shard_map/while/body/eval_jaxpr/zyx,kx->zyk/dot_general | solution.py:32
  105.7 9.6 %fusion.161 = f32[4,16,2048]{2,1,0:T(8,128)S(1)} fusion(f32[4,16,2048]{2,1,0:T(8,128)S(1)} %get-tuple-element.753, s32[]{:T(128)S(6)} %select_n.174, f32[4,16,2048]{2,1,0:T(8,128)S(1)} %get-tuple-element.761, s32[2048]{0:T(1024)S(1)} %fusion.160, s32[256]{0:T(256)S(1)} %iota_add_fusion.2, f32[256]{0:T(256)S(1)} %compare_select_fusion.3), kind=kOutput, calls=%fused_computation.19.clone.1 | convolution fusion | flops 410517504 | bytes 600068 | tf_op jit(solution)/shard_map/while/body/eval_jaxpr/zyx,kx->zyk/dot_general | solution.py:32
  123.8 9.5 %all-to-all-start.1 = ((f32[16,1,8192]{2,1,0:T(1,128)}), f32[16,1,8192]{2,1,0:T(1,128)S(1)}, u32[]{:S(2)}, u32[]{:S(2)}) async-start(f32[16,1,8192]{2,1,0:T(1,128)} %reshape.128), calls=%async_computation.1 | async-start | bytes 1048576 | tf_op jit(solution)/shard_map/all_to_all | solution.py:90
  133.5 17.2 %all-to-all-done.1 = f32[16,1,8192]{2,1,0:T(1,128)S(1)} async-done(((f32[16,1,8192]{2,1,0:T(1,128)}), f32[16,1,8192]{2,1,0:T(1,128)S(1)}, u32[]{:S(2)}, u32[]{:S(2)}) %all-to-all-start.1) | async-done | bytes 524320 | tf_op jit(solution)/shard_map/all_to_all | solution.py:90
  160.5 26.0 %while.69 = (s32[]{:T(128)}, f32[4,128]{1,0:T(4,128)S(1)}, f32[4,128]{1,0:T(4,128)S(1)}, f32[32,8,4,128]{3,2,1,0:T(4,128)S(1)}, f32[32,8,4,128]{3,2,1,0:T(4,128)...) while((s32[]{:T(128)}, f32[4,128]{1,0:T(4,128)S(1)}, ...), condition=%wide.region_3.4_spmd.clone, body=%wide.region_2.3_spmd.clone.sunk | while | flops 33288 | bytes 220976 | solution.py:65
  187.5 23.0 %while.70 = (s32[]{:T(128)}, f32[4,128]{1,0:T(4,128)S(1)}, f32[32,8,4,128]{3,2,1,0:T(4,128)}, f32[32,8,4,128]{3,2,1,0:T(4,128)S(1)}, f32[32,8,4,128]{3,2,1,0:T(4...) while((s32[]{:T(128)}, f32[4,128]{1,0:T(4,128)S(1)}, ...), condition=%wide.region_5.6_spmd.clone, body=%wide.region_4.5_spmd.clone.sunk | while | flops 8714 | bytes 114971 | solution.py:73
  210.5 12.1 %all-to-all-start.2 = ((f32[4,256,128]{2,0,1:T(4,128)}), f32[4,256,128]{2,0,1:T(4,128)S(1)}, u32[]{:S(2)}, u32[]{:S(2)}) async-start(f32[4,256,128]{2,0,1:T(4,128)} %bitcast.11), calls=%async_computation.2 | async-start | bytes 1048576 | tf_op jit(solution)/shard_map/all_to_all | solution.py:96
  222.6 16.5 %all-to-all-done.2 = f32[4,256,128]{2,0,1:T(4,128)S(1)} async-done(((f32[4,256,128]{2,0,1:T(4,128)}), f32[4,256,128]{2,0,1:T(4,128)S(1)}, u32[]{:S(2)}, u32[]{:S(2)}) %all-to-all-start.2) | async-done | bytes 524320 | tf_op jit(solution)/shard_map/all_to_all | solution.py:96
  239.6 73.0 %while.68 = (s32[]{:T(128)}, f32[4,16,2048]{2,1,0:T(8,128)S(1)}, f32[4,16,2048]{2,1,0:T(8,128)S(1)}, s32[]{:T(128)}, s32[]{:T(128)}, /*index=5*/s32[]{:T(128)}, s32[]{:T(128)}) while((s32[]{:T(128)}, f32[4,16,2048]{2,1,0:T(8,128)S(1)}, f32[4,16,2048]{2,1,0:T(8,128)S(1)}, s32[]{:T(128)}, s32[]{:T(128)}, ...), condition=%wide.region_7.8_spmd.clone.clone, body=%wide.region_6.7_spmd.clone.clone.sunk | while | flops 410522368 | bytes 608387 | solution.py:51
  248.7 9.1 %fusion.165 = f32[4,16,2048]{2,1,0:T(8,128)S(1)} fusion(f32[4,16,2048]{2,1,0:T(8,128)S(1)} %get-tuple-element.870, s32[]{:T(128)S(6)} %select_n.177, f32[4,16,2048]{2,1,0:T(8,128)S(1)} %get-tuple-element.878, s32[256]{0:T(256)S(1)} %multiply_add_fusion.3, f32[2048]{0:T(1024)S(1)} %fusion.164), kind=kOutput, calls=%fused_computation.50.clone.1 | convolution fusion | flops 410517504 | bytes 599044 | tf_op jit(solution)/shard_map/while/body/eval_jaxpr/zyk,kx->zyx/dot_general | solution.py:48
  257.9 9.1 %fusion.165 = f32[4,16,2048]{2,1,0:T(8,128)S(1)} fusion(f32[4,16,2048]{2,1,0:T(8,128)S(1)} %get-tuple-element.870, s32[]{:T(128)S(6)} %select_n.177, f32[4,16,2048]{2,1,0:T(8,128)S(1)} %get-tuple-element.878, s32[256]{0:T(256)S(1)} %multiply_add_fusion.3, f32[2048]{0:T(1024)S(1)} %fusion.164), kind=kOutput, calls=%fused_computation.50.clone.1 | convolution fusion | flops 410517504 | bytes 599044 | tf_op jit(solution)/shard_map/while/body/eval_jaxpr/zyk,kx->zyx/dot_general | solution.py:48
  276.1 9.1 %fusion.165 = f32[4,16,2048]{2,1,0:T(8,128)S(1)} fusion(f32[4,16,2048]{2,1,0:T(8,128)S(1)} %get-tuple-element.870, s32[]{:T(128)S(6)} %select_n.177, f32[4,16,2048]{2,1,0:T(8,128)S(1)} %get-tuple-element.878, s32[256]{0:T(256)S(1)} %multiply_add_fusion.3, f32[2048]{0:T(1024)S(1)} %fusion.164), kind=kOutput, calls=%fused_computation.50.clone.1 | convolution fusion | flops 410517504 | bytes 599044 | tf_op jit(solution)/shard_map/while/body/eval_jaxpr/zyk,kx->zyx/dot_general | solution.py:48
  294.4 9.1 %fusion.165 = f32[4,16,2048]{2,1,0:T(8,128)S(1)} fusion(f32[4,16,2048]{2,1,0:T(8,128)S(1)} %get-tuple-element.870, s32[]{:T(128)S(6)} %select_n.177, f32[4,16,2048]{2,1,0:T(8,128)S(1)} %get-tuple-element.878, s32[256]{0:T(256)S(1)} %multiply_add_fusion.3, f32[2048]{0:T(1024)S(1)} %fusion.164), kind=kOutput, calls=%fused_computation.50.clone.1 | convolution fusion | flops 410517504 | bytes 599044 | tf_op jit(solution)/shard_map/while/body/eval_jaxpr/zyk,kx->zyx/dot_general | solution.py:48
  303.5 9.1 %fusion.165 = f32[4,16,2048]{2,1,0:T(8,128)S(1)} fusion(f32[4,16,2048]{2,1,0:T(8,128)S(1)} %get-tuple-element.870, s32[]{:T(128)S(6)} %select_n.177, f32[4,16,2048]{2,1,0:T(8,128)S(1)} %get-tuple-element.878, s32[256]{0:T(256)S(1)} %multiply_add_fusion.3, f32[2048]{0:T(1024)S(1)} %fusion.164), kind=kOutput, calls=%fused_computation.50.clone.1 | convolution fusion | flops 410517504 | bytes 599044 | tf_op jit(solution)/shard_map/while/body/eval_jaxpr/zyk,kx->zyx/dot_general | solution.py:48
  320.4 21.3 %all_to_all.72 = f32[32,1,4096]{2,1,0:T(1,128)S(1)} all-to-all(f32[32,1,4096]{2,1,0:T(1,128)S(1)} %reshape.130), channel_id=1, replica_groups=mesh['gx'=32,'gy'=16] {'gx'}, dimensions={0} | all-to-all | bytes 1048576 | tf_op jit(solution)/shard_map/all_to_all | solution.py:100
  (816 shorter events, 121.3 us)
Async XLA Ops:
  0.0 1.0 copy-start
  3.9 30.0 %all-to-all-start = ((f32[32,1,4096]{2,1,0:T(1,128)}), f32[32,1,4096]{2,1,0:T(1,128)S(1)}, u32[]{:S(2)}, u32[]{:S(2)}) async-start(f32[32,1,4096]{2,1,0:T(1,128)} %reshape.126), calls=%async_computation | async-start | bytes 1048576 | tf_op jit(solution)/shard_map/all_to_all | solution.py:86
  123.8 26.8 %all-to-all-start.1 = ((f32[16,1,8192]{2,1,0:T(1,128)}), f32[16,1,8192]{2,1,0:T(1,128)S(1)}, u32[]{:S(2)}, u32[]{:S(2)}) async-start(f32[16,1,8192]{2,1,0:T(1,128)} %reshape.128), calls=%async_computation.1 | async-start | bytes 1048576 | tf_op jit(solution)/shard_map/all_to_all | solution.py:90
  210.5 28.6 %all-to-all-start.2 = ((f32[4,256,128]{2,0,1:T(4,128)}), f32[4,256,128]{2,0,1:T(4,128)S(1)}, u32[]{:S(2)}, u32[]{:S(2)}) async-start(f32[4,256,128]{2,0,1:T(4,128)} %bitcast.11), calls=%async_computation.2 | async-start | bytes 1048576 | tf_op jit(solution)/shard_map/all_to_all | solution.py:96
where the time goes:
time: 359 us; the launch traced here: 354 us
  matrix products  151 us (42%)
  local copies, waits for them, and re-layouts  64.1 us (18%)
  waiting for transfers between devices  50 us (14%)
  starting transfers between devices  35.4 us (10%)
  other arithmetic  28.3 us (8%)
  blocking collectives  21.3 us (6%)
    dot_general x8, matrix products, forward_one_block(): piece = jnp.einsum('zyx,kx->zyk', received, cos_table, precision=highest)  76.7 us
    dot_general x8, matrix products, backward_one_block(): piece = jnp.einsum('zyk,kx->zyx', solved, cos_table, precision=highest)  72.7 us
    unnamed x8, local copies, waits for them, and re-layouts  21.6 us
    all_to_all x1, blocking collectives, shards(): lax.all_to_all(physical, 'gx', split_axis=2, concat_axis=0, tiled=True)  21.3 us
    dynamic_update_slice x64, local copies, waits for them, and re-layouts, thomas(): lax.scan(forward_step, (empty_line, empty_line), rhs_lines, unroll=8)  20.1 us
    while x256, other arithmetic  19.5 us
    all_to_all x1, waiting for transfers between devices, shards(): lax.all_to_all(spectral, 'gy', split_axis=2, concat_axis=1, tiled=True)  17.2 us
    all_to_all x1, waiting for transfers between devices, shards(): lax.all_to_all(jnp.moveaxis(solved_columns, 0, 1), 'gy', split_axis=1, co...  16.5 us
  transfers between devices with their start and end apart: 3, of which 3 were waited for; matrix products, arithmetic and copies ran while one was open for 0% of the time, Pallas kernels for 0%

commit v1 on v0

--- a/solution.py
+++ b/solution.py
@@ -6,6 +6,22 @@
 
 SCREEN = 32
 highest = lax.Precision.HIGHEST
+
+
+def pairwise_exchange(value, axis, split, join):
+    ways, here = (lax.axis_size(axis), lax.axis_index(axis))
+    width = value.shape[split] // ways
+    shape = list(value.shape)
+    shape[split] = width
+    height = shape[join]
+    shape[join] = height * ways
+    full = jnp.zeros(shape, value.dtype)
+    for mask in range(ways):
+        part = lax.dynamic_slice_in_dim(value, (here ^ mask) * width, width, axis=split)
+        if mask:
+            part = lax.ppermute(part, axis, [(d, d ^ mask) for d in range(ways)])
+        full = lax.dynamic_update_slice_in_dim(full, part, (here ^ mask) * height, axis=join)
+    return full
 
 
 def cosine_table(points, wavenums, places):
@@ -93,9 +109,7 @@
     x_eigen = eigenvalue(column_first + jnp.arange(column_count, dtype=jnp.int32), nx_cells)
     diagonal = 2.0 + (screen_shift + z_eigen[:, None] + x_eigen[None, :])
     solved_columns = thomas(jnp.moveaxis(columns, 1, 0), diagonal)
-    solved = lax.all_to_all(
-        jnp.moveaxis(solved_columns, 0, 1), "gy", split_axis=1, concat_axis=2, tiled=True
-    )
+    solved = pairwise_exchange(jnp.moveaxis(solved_columns, 0, 1), "gy", 1, 2)
     physical = backward_cosine(solved)
     regrouped = lax.all_to_all(physical, "gx", split_axis=2, concat_axis=0, tiled=True)
     return jnp.einsum("kyx,kz->xyz", regrouped, z_table, precision=highest)

time: 359 us -> 382 us (1.064)
  starting transfers between devices: 35.4 us -> 89 us
  local copies, waits for them, and re-layouts: 64.1 us -> 44.2 us
  waiting for transfers between devices: 50 us -> 34.6 us
    ppermute x0 -> x15, starting transfers between devices: none -> 54.2 us  [pairwise_exchange(): part = lax.ppermute(part, axis, [(d, d ^ mask) for d in range(ways)])]
    dynamic_update_slice x64, local copies, waits for them, and re-layouts: 20.1 us -> 0.99 us  [thomas(): lax.scan(forward_step, (empty_line, empty_line), rhs_lines, unroll=8)]
    all_to_all x1 -> x0, waiting for transfers between devices: 16.5 us -> none  [shards(): lax.all_to_all(jnp.moveaxis(solved_columns, 0, 1), 'gy', split_axis=1, co...]
    all_to_all x1 -> x0, starting transfers between devices: 12.1 us -> none  [shards(): lax.all_to_all(jnp.moveaxis(solved_columns, 0, 1), 'gy', split_axis=1, co...]
    all_to_all x1, starting transfers between devices: 9.5 us -> 21.1 us  [shards(): lax.all_to_all(spectral, 'gy', split_axis=2, concat_axis=1, tiled=True)]
    unnamed x8 -> x23, local copies, waits for them, and re-layouts: 21.6 us -> 21.7 us
  transfers between devices with their start and end apart: 3 -> 17, of which waited for: 3 -> 3; matrix products, arithmetic and copies ran while one was open for 0% -> 0% of each run, Pallas kernels for 0% -> 0%
where the time goes in v1:
time: 382 us; the launch traced here: 374 us
  matrix products  151 us (40%)
  starting transfers between devices  89 us (23%)
  local copies, waits for them, and re-layouts  44.2 us (12%)
  waiting for transfers between devices  34.6 us (9%)
  other arithmetic  29 us (8%)
  blocking collectives  21 us (5%)
  loops' own time  4.22 us (1%)
    dot_general x8, matrix products, forward_one_block(): piece = jnp.einsum('zyx,kx->zyk', received, cos_table, precision=highest)  76.7 us
    dot_general x8, matrix products, backward_one_block(): piece = jnp.einsum('zyk,kx->zyx', solved, cos_table, precision=highest)  72.6 us
    ppermute x15, starting transfers between devices, pairwise_exchange(): part = lax.ppermute(part, axis, [(d, d ^ mask) for d in range(ways)])  54.2 us
    unnamed x23, local copies, waits for them, and re-layouts  21.7 us
    all_to_all x1, starting transfers between devices, shards(): lax.all_to_all(spectral, 'gy', split_axis=2, concat_axis=1, tiled=True)  21.1 us
    all_to_all x1, blocking collectives, shards(): lax.all_to_all(physical, 'gx', split_axis=2, concat_axis=0, tiled=True)  21 us
    while x256, other arithmetic  20.3 us
    all_to_all x1, waiting for transfers between devices, shards(): lax.all_to_all(spectral, 'gy', split_axis=2, concat_axis=1, tiled=True)  16.8 us
  transfers between devices with their start and end apart: 17, of which 3 were waited for; matrix products, arithmetic and copies ran while one was open for 0% of the time, Pallas kernels for 0%

profile of v1, /device:TPU:1, one launch (start us, length us, event | category | flops | bytes accessed | tf_op | source)
XLA Modules:
  0.0 374.2 jit_solution(8184484392525721907)
XLA Ops:
  3.9 13.7 %all-to-all-start = ((f32[32,1,4096]{2,1,0:T(1,128)}), f32[32,1,4096]{2,1,0:T(1,128)S(1)}, u32[]{:S(2)}, u32[]{:S(2)}) async-start(f32[32,1,4096]{2,1,0:T(1,128)} %reshape.126), calls=%async_computation | async-start | bytes 1048576 | tf_op jit(solution)/shard_map/all_to_all | solution.py:102
  17.6 16.3 %all-to-all-done = f32[32,1,4096]{2,1,0:T(1,128)S(1)} async-done(((f32[32,1,4096]{2,1,0:T(1,128)}), f32[32,1,4096]{2,1,0:T(1,128)S(1)}, u32[]{:S(2)}, u32[]{:S(2)}) %all-to-all-start) | async-done | bytes 524320 | tf_op jit(solution)/shard_map/all_to_all | solution.py:102
  37.8 77.5 %while.67 = (s32[]{:T(128)}, f32[4,16,2048]{2,1,0:T(8,128)S(1)}, f32[4,16,2048]{2,1,0:T(8,128)S(1)}, s32[]{:T(128)}, s32[]{:T(128)}, /*index=5*/s32[]{:T(128)}, s32[]{:T(128)}) while((s32[]{:T(128)}, f32[4,16,2048]{2,1,0:T(8,128)S(1)}, f32[4,16,2048]{2,1,0:T(8,128)S(1)}, s32[]{:T(128)}, s32[]{:T(128)}, /*index=5*/s32[]{:T(128)}, ...), condition=%wide.region_1.2_spmd.clone, body=%wide.region_0.1_spmd.clone.sunk | while | flops 410522624 | bytes 610439 | solution.py:51
  38.2 9.6 %fusion.162 = f32[4,16,2048]{2,1,0:T(8,128)S(1)} fusion(f32[4,16,2048]{2,1,0:T(8,128)S(1)} %get-tuple-element.769, s32[]{:T(128)S(6)} %select_n.302, f32[4,16,2048]{2,1,0:T(8,128)S(1)} %get-tuple-element.777, s32[2048]{0:T(1024)S(1)} %fusion.161, s32[256]{0:T(256)S(1)} %iota_add_fusion.2, f32[256]{0:T(256)S(1)} %compare_select_fusion.3), kind=kOutput, calls=%fused_computation.19.clone.1 | convolution fusion | flops 410517504 | bytes 600068 | tf_op jit(solution)/shard_map/while/body/eval_jaxpr/zyx,kx->zyk/dot_general | solution.py:48
  47.8 9.6 %fusion.162 = f32[4,16,2048]{2,1,0:T(8,128)S(1)} fusion(f32[4,16,2048]{2,1,0:T(8,128)S(1)} %get-tuple-element.769, s32[]{:T(128)S(6)} %select_n.302, f32[4,16,2048]{2,1,0:T(8,128)S(1)} %get-tuple-element.777, s32[2048]{0:T(1024)S(1)} %fusion.161, s32[256]{0:T(256)S(1)} %iota_add_fusion.2, f32[256]{0:T(256)S(1)} %compare_select_fusion.3), kind=kOutput, calls=%fused_computation.19.clone.1 | convolution fusion | flops 410517504 | bytes 600068 | tf_op jit(solution)/shard_map/while/body/eval_jaxpr/zyx,kx->zyk/dot_general | solution.py:48
  57.5 9.6 %fusion.162 = f32[4,16,2048]{2,1,0:T(8,128)S(1)} fusion(f32[4,16,2048]{2,1,0:T(8,128)S(1)} %get-tuple-element.769, s32[]{:T(128)S(6)} %select_n.302, f32[4,16,2048]{2,1,0:T(8,128)S(1)} %get-tuple-element.777, s32[2048]{0:T(1024)S(1)} %fusion.161, s32[256]{0:T(256)S(1)} %iota_add_fusion.2, f32[256]{0:T(256)S(1)} %compare_select_fusion.3), kind=kOutput, calls=%fused_computation.19.clone.1 | convolution fusion | flops 410517504 | bytes 600068 | tf_op jit(solution)/shard_map/while/body/eval_jaxpr/zyx,kx->zyk/dot_general | solution.py:48
  67.1 9.6 %fusion.162 = f32[4,16,2048]{2,1,0:T(8,128)S(1)} fusion(f32[4,16,2048]{2,1,0:T(8,128)S(1)} %get-tuple-element.769, s32[]{:T(128)S(6)} %select_n.302, f32[4,16,2048]{2,1,0:T(8,128)S(1)} %get-tuple-element.777, s32[2048]{0:T(1024)S(1)} %fusion.161, s32[256]{0:T(256)S(1)} %iota_add_fusion.2, f32[256]{0:T(256)S(1)} %compare_select_fusion.3), kind=kOutput, calls=%fused_computation.19.clone.1 | convolution fusion | flops 410517504 | bytes 600068 | tf_op jit(solution)/shard_map/while/body/eval_jaxpr/zyx,kx->zyk/dot_general | solution.py:48
  76.8 9.6 %fusion.162 = f32[4,16,2048]{2,1,0:T(8,128)S(1)} fusion(f32[4,16,2048]{2,1,0:T(8,128)S(1)} %get-tuple-element.769, s32[]{:T(128)S(6)} %select_n.302, f32[4,16,2048]{2,1,0:T(8,128)S(1)} %get-tuple-element.777, s32[2048]{0:T(1024)S(1)} %fusion.161, s32[256]{0:T(256)S(1)} %iota_add_fusion.2, f32[256]{0:T(256)S(1)} %compare_select_fusion.3), kind=kOutput, calls=%fused_computation.19.clone.1 | convolution fusion | flops 410517504 | bytes 600068 | tf_op jit(solution)/shard_map/while/body/eval_jaxpr/zyx,kx->zyk/dot_general | solution.py:48
  86.4 9.6 %fusion.162 = f32[4,16,2048]{2,1,0:T(8,128)S(1)} fusion(f32[4,16,2048]{2,1,0:T(8,128)S(1)} %get-tuple-element.769, s32[]{:T(128)S(6)} %select_n.302, f32[4,16,2048]{2,1,0:T(8,128)S(1)} %get-tuple-element.777, s32[2048]{0:T(1024)S(1)} %fusion.161, s32[256]{0:T(256)S(1)} %iota_add_fusion.2, f32[256]{0:T(256)S(1)} %compare_select_fusion.3), kind=kOutput, calls=%fused_computation.19.clone.1 | convolution fusion | flops 410517504 | bytes 600068 | tf_op jit(solution)/shard_map/while/body/eval_jaxpr/zyx,kx->zyk/dot_general | solution.py:48
  96.1 9.6 %fusion.162 = f32[4,16,2048]{2,1,0:T(8,128)S(1)} fusion(f32[4,16,2048]{2,1,0:T(8,128)S(1)} %get-tuple-element.769, s32[]{:T(128)S(6)} %select_n.302, f32[4,16,2048]{2,1,0:T(8,128)S(1)} %get-tuple-element.777, s32[2048]{0:T(1024)S(1)} %fusion.161, s32[256]{0:T(256)S(1)} %iota_add_fusion.2, f32[256]{0:T(256)S(1)} %compare_select_fusion.3), kind=kOutput, calls=%fused_computation.19.clone.1 | convolution fusion | flops 410517504 | bytes 600068 | tf_op jit(solution)/shard_map/while/body/eval_jaxpr/zyx,kx->zyk/dot_general | solution.py:48
  105.7 9.6 %fusion.162 = f32[4,16,2048]{2,1,0:T(8,128)S(1)} fusion(f32[4,16,2048]{2,1,0:T(8,128)S(1)} %get-tuple-element.769, s32[]{:T(128)S(6)} %select_n.302, f32[4,16,2048]{2,1,0:T(8,128)S(1)} %get-tuple-element.777, s32[2048]{0:T(1024)S(1)} %fusion.161, s32[256]{0:T(256)S(1)} %iota_add_fusion.2, f32[256]{0:T(256)S(1)} %compare_select_fusion.3), kind=kOutput, calls=%fused_computation.19.clone.1 | convolution fusion | flops 410517504 | bytes 600068 | tf_op jit(solution)/shard_map/while/body/eval_jaxpr/zyx,kx->zyk/dot_general | solution.py:48
  123.8 21.1 %all-to-all-start.1 = ((f32[16,1,8192]{2,1,0:T(1,128)}), f32[16,1,8192]{2,1,0:T(1,128)S(1)}, u32[]{:S(2)}, u32[]{:S(2)}) async-start(f32[16,1,8192]{2,1,0:T(1,128)} %reshape.128), calls=%async_computation.1 | async-start | bytes 1048576 | tf_op jit(solution)/shard_map/all_to_all | solution.py:106
  145.3 16.8 %all-to-all-done.1 = f32[16,1,8192]{2,1,0:T(1,128)S(1)} async-done(((f32[16,1,8192]{2,1,0:T(1,128)}), f32[16,1,8192]{2,1,0:T(1,128)S(1)}, u32[]{:S(2)}, u32[]{:S(2)}) %all-to-all-start.1) | async-done | bytes 524320 | tf_op jit(solution)/shard_map/all_to_all | solution.py:106
  171.9 26.0 %while.69 = (s32[]{:T(128)}, f32[4,128]{1,0:T(4,128)S(1)}, f32[4,128]{1,0:T(4,128)S(1)}, f32[32,8,4,128]{3,2,1,0:T(4,128)S(1)}, f32[32,8,4,128]{3,2,1,0:T(4,128)...) while((s32[]{:T(128)}, f32[4,128]{1,0:T(4,128)S(1)}, ...), condition=%wide.region_3.4_spmd.clone, body=%wide.region_2.3_spmd.clone.sunk | while | flops 33288 | bytes 220976 | solution.py:81
  260.1 73.0 %while.68 = (s32[]{:T(128)}, f32[4,16,2048]{2,1,0:T(8,128)S(1)}, f32[4,16,2048]{2,1,0:T(8,128)S(1)}, s32[]{:T(128)}, s32[]{:T(128)}, /*index=5*/s32[]{:T(128)}, s32[]{:T(128)}) while((s32[]{:T(128)}, f32[4,16,2048]{2,1,0:T(8,128)S(1)}, f32[4,16,2048]{2,1,0:T(8,128)S(1)}, s32[]{:T(128)}, s32[]{:T(128)}, ...), condition=%wide.region_7.8_spmd.clone.clone, body=%wide.region_6.7_spmd.clone.clone.sunk | while | flops 410522368 | bytes 608387 | solution.py:67
  260.1 9.1 %fusion.166 = f32[4,16,2048]{2,1,0:T(8,128)S(1)} fusion(f32[4,16,2048]{2,1,0:T(8,128)S(1)} %get-tuple-element.886, s32[]{:T(128)S(6)} %select_n.305, f32[4,16,2048]{2,1,0:T(8,128)S(1)} %get-tuple-element.894, s32[256]{0:T(256)S(1)} %multiply_add_fusion.3, f32[2048]{0:T(1024)S(1)} %fusion.165), kind=kOutput, calls=%fused_computation.50.clone.1 | convolution fusion | flops 410517504 | bytes 599044 | tf_op jit(solution)/shard_map/while/body/eval_jaxpr/zyk,kx->zyx/dot_general | solution.py:64
  269.3 9.1 %fusion.166 = f32[4,16,2048]{2,1,0:T(8,128)S(1)} fusion(f32[4,16,2048]{2,1,0:T(8,128)S(1)} %get-tuple-element.886, s32[]{:T(128)S(6)} %select_n.305, f32[4,16,2048]{2,1,0:T(8,128)S(1)} %get-tuple-element.894, s32[256]{0:T(256)S(1)} %multiply_add_fusion.3, f32[2048]{0:T(1024)S(1)} %fusion.165), kind=kOutput, calls=%fused_computation.50.clone.1 | convolution fusion | flops 410517504 | bytes 599044 | tf_op jit(solution)/shard_map/while/body/eval_jaxpr/zyk,kx->zyx/dot_general | solution.py:64
  278.4 9.1 %fusion.166 = f32[4,16,2048]{2,1,0:T(8,128)S(1)} fusion(f32[4,16,2048]{2,1,0:T(8,128)S(1)} %get-tuple-element.886, s32[]{:T(128)S(6)} %select_n.305, f32[4,16,2048]{2,1,0:T(8,128)S(1)} %get-tuple-element.894, s32[256]{0:T(256)S(1)} %multiply_add_fusion.3, f32[2048]{0:T(1024)S(1)} %fusion.165), kind=kOutput, calls=%fused_computation.50.clone.1 | convolution fusion | flops 410517504 | bytes 599044 | tf_op jit(solution)/shard_map/while/body/eval_jaxpr/zyk,kx->zyx/dot_general | solution.py:64
  287.5 9.1 %fusion.166 = f32[4,16,2048]{2,1,0:T(8,128)S(1)} fusion(f32[4,16,2048]{2,1,0:T(8,128)S(1)} %get-tuple-element.886, s32[]{:T(128)S(6)} %select_n.305, f32[4,16,2048]{2,1,0:T(8,128)S(1)} %get-tuple-element.894, s32[256]{0:T(256)S(1)} %multiply_add_fusion.3, f32[2048]{0:T(1024)S(1)} %fusion.165), kind=kOutput, calls=%fused_computation.50.clone.1 | convolution fusion | flops 410517504 | bytes 599044 | tf_op jit(solution)/shard_map/while/body/eval_jaxpr/zyk,kx->zyx/dot_general | solution.py:64
  296.6 9.1 %fusion.166 = f32[4,16,2048]{2,1,0:T(8,128)S(1)} fusion(f32[4,16,2048]{2,1,0:T(8,128)S(1)} %get-tuple-element.886, s32[]{:T(128)S(6)} %select_n.305, f32[4,16,2048]{2,1,0:T(8,128)S(1)} %get-tuple-element.894, s32[256]{0:T(256)S(1)} %multiply_add_fusion.3, f32[2048]{0:T(1024)S(1)} %fusion.165), kind=kOutput, calls=%fused_computation.50.clone.1 | convolution fusion | flops 410517504 | bytes 599044 | tf_op jit(solution)/shard_map/while/body/eval_jaxpr/zyk,kx->zyx/dot_general | solution.py:64
  305.8 9.1 %fusion.166 = f32[4,16,2048]{2,1,0:T(8,128)S(1)} fusion(f32[4,16,2048]{2,1,0:T(8,128)S(1)} %get-tuple-element.886, s32[]{:T(128)S(6)} %select_n.305, f32[4,16,2048]{2,1,0:T(8,128)S(1)} %get-tuple-element.894, s32[256]{0:T(256)S(1)} %multiply_add_fusion.3, f32[2048]{0:T(1024)S(1)} %fusion.165), kind=kOutput, calls=%fused_computation.50.clone.1 | convolution fusion | flops 410517504 | bytes 599044 | tf_op jit(solution)/shard_map/while/body/eval_jaxpr/zyk,kx->zyx/dot_general | solution.py:64
  314.9 9.1 %fusion.166 = f32[4,16,2048]{2,1,0:T(8,128)S(1)} fusion(f32[4,16,2048]{2,1,0:T(8,128)S(1)} %get-tuple-element.886, s32[]{:T(128)S(6)} %select_n.305, f32[4,16,2048]{2,1,0:T(8,128)S(1)} %get-tuple-element.894, s32[256]{0:T(256)S(1)} %multiply_add_fusion.3, f32[2048]{0:T(1024)S(1)} %fusion.165), kind=kOutput, calls=%fused_computation.50.clone.1 | convolution fusion | flops 410517504 | bytes 599044 | tf_op jit(solution)/shard_map/while/body/eval_jaxpr/zyk,kx->zyx/dot_general | solution.py:64
  324.0 9.1 %fusion.166 = f32[4,16,2048]{2,1,0:T(8,128)S(1)} fusion(f32[4,16,2048]{2,1,0:T(8,128)S(1)} %get-tuple-element.886, s32[]{:T(128)S(6)} %select_n.305, f32[4,16,2048]{2,1,0:T(8,128)S(1)} %get-tuple-element.894, s32[256]{0:T(256)S(1)} %multiply_add_fusion.3, f32[2048]{0:T(1024)S(1)} %fusion.165), kind=kOutput, calls=%fused_computation.50.clone.1 | convolution fusion | flops 410517504 | bytes 599044 | tf_op jit(solution)/shard_map/while/body/eval_jaxpr/zyk,kx->zyx/dot_general | solution.py:64
  340.9 21.0 %all_to_all.54 = f32[32,1,4096]{2,1,0:T(1,128)S(1)} all-to-all(f32[32,1,4096]{2,1,0:T(1,128)S(1)} %reshape.130), channel_id=1, replica_groups=mesh['gx'=32,'gy'=16] {'gx'}, dimensions={0} | all-to-all | bytes 1048576 | tf_op jit(solution)/shard_map/all_to_all | solution.py:114
  (875 shorter events, 136.0 us)
Async XLA Ops:
  0.0 1.0 copy-start
  3.9 30.0 %all-to-all-start = ((f32[32,1,4096]{2,1,0:T(1,128)}), f32[32,1,4096]{2,1,0:T(1,128)S(1)}, u32[]{:S(2)}, u32[]{:S(2)}) async-start(f32[32,1,4096]{2,1,0:T(1,128)} %reshape.126), calls=%async_computation | async-start | bytes 1048576 | tf_op jit(solution)/shard_map/all_to_all | solution.py:102
  123.8 38.3 %all-to-all-start.1 = ((f32[16,1,8192]{2,1,0:T(1,128)}), f32[16,1,8192]{2,1,0:T(1,128)S(1)}, u32[]{:S(2)}, u32[]{:S(2)}) async-start(f32[16,1,8192]{2,1,0:T(1,128)} %reshape.128), calls=%async_computation.1 | async-start | bytes 1048576 | tf_op jit(solution)/shard_map/all_to_all | solution.py:106
  203.7 14.2 %collective-permute-start = (f32[4,16,128]{2,1,0:T(8,128)S(1)}, f32[4,16,128]{2,1,0:T(8,128)S(1)}, u32[]{:S(2)}, u32[]{:S(2)}) collective-permute-start(f32[4,16,128]{2,1,0:T(8,128)S(1)} %bitcast.387), channel_id=1, source_target_pairs={{0,1},{1,0},{2,3},{3,2},{4,5},{5,4},{6,7},{7,6},{8,9},{9,8},{10,11... | collective-permute-start | bytes 98312 | tf_op jit(solution)/shard_map/ppermute | solution.py:22
  205.6 15.5 %collective-permute-start.1 = (f32[4,16,128]{2,1,0:T(8,128)S(1)}, f32[4,16,128]{2,1,0:T(8,128)S(1)}, u32[]{:S(2)}, u32[]{:S(2)}) collective-permute-start(f32[4,16,128]{2,1,0:T(8,128)S(1)} %bitcast.386), channel_id=1, source_target_pairs={{0,2},{1,3},{2,0},{3,1},{4,6},{5,7},{6,4},{7,5},{8,10},{9,11},{10,... | collective-permute-start | bytes 98312 | tf_op jit(solution)/shard_map/ppermute | solution.py:22
  207.6 18.2 %collective-permute-start.2 = (f32[4,16,128]{2,1,0:T(8,128)S(1)}, f32[4,16,128]{2,1,0:T(8,128)S(1)}, u32[]{:S(2)}, u32[]{:S(2)}) collective-permute-start(f32[4,16,128]{2,1,0:T(8,128)S(1)} %bitcast.385), channel_id=1, source_target_pairs={{0,3},{1,2},{2,1},{3,0},{4,7},{5,6},{6,5},{7,4},{8,11},{9,10},{10,... | collective-permute-start | bytes 98312 | tf_op jit(solution)/shard_map/ppermute | solution.py:22
  211.6 17.0 %collective-permute-start.3 = (f32[4,16,128]{2,1,0:T(8,128)S(1)}, f32[4,16,128]{2,1,0:T(8,128)S(1)}, u32[]{:S(2)}, u32[]{:S(2)}) collective-permute-start(f32[4,16,128]{2,1,0:T(8,128)S(1)} %bitcast.384), channel_id=1, source_target_pairs={{0,4},{1,5},{2,6},{3,7},{4,0},{5,1},{6,2},{7,3},{8,12},{9,13},{10,... | collective-permute-start | bytes 98312 | tf_op jit(solution)/shard_map/ppermute | solution.py:22
  213.6 21.3 %collective-permute-start.4 = (f32[4,16,128]{2,1,0:T(8,128)S(1)}, f32[4,16,128]{2,1,0:T(8,128)S(1)}, u32[]{:S(2)}, u32[]{:S(2)}) collective-permute-start(f32[4,16,128]{2,1,0:T(8,128)S(1)} %bitcast.383), channel_id=1, source_target_pairs={{0,5},{1,4},{2,7},{3,6},{4,1},{5,0},{6,3},{7,2},{8,13},{9,12},{10,... | collective-permute-start | bytes 98312 | tf_op jit(solution)/shard_map/ppermute | solution.py:22
  217.9 18.9 %collective-permute-start.5 = (f32[4,16,128]{2,1,0:T(8,128)S(1)}, f32[4,16,128]{2,1,0:T(8,128)S(1)}, u32[]{:S(2)}, u32[]{:S(2)}) collective-permute-start(f32[4,16,128]{2,1,0:T(8,128)S(1)} %bitcast.382), channel_id=1, source_target_pairs={{0,6},{1,7},{2,4},{3,5},{4,2},{5,3},{6,0},{7,1},{8,14},{9,15},{10,... | collective-permute-start | bytes 98312 | tf_op jit(solution)/shard_map/ppermute | solution.py:22
  221.1 22.8 %collective-permute-start.6 = (f32[4,16,128]{2,1,0:T(8,128)S(1)}, f32[4,16,128]{2,1,0:T(8,128)S(1)}, u32[]{:S(2)}, u32[]{:S(2)}) collective-permute-start(f32[4,16,128]{2,1,0:T(8,128)S(1)} %bitcast.381), channel_id=1, source_target_pairs={{0,7},{1,6},{2,5},{3,4},{4,3},{5,2},{6,1},{7,0},{8,15},{9,14},{10,... | collective-permute-start | bytes 98312 | tf_op jit(solution)/shard_map/ppermute | solution.py:22
  225.7 20.1 %collective-permute-start.7 = (f32[4,16,128]{2,1,0:T(8,128)S(1)}, f32[4,16,128]{2,1,0:T(8,128)S(1)}, u32[]{:S(2)}, u32[]{:S(2)}) collective-permute-start(f32[4,16,128]{2,1,0:T(8,128)S(1)} %bitcast.380), channel_id=1, source_target_pairs={{0,8},{1,9},{2,10},{3,11},{4,12},{5,13},{6,14},{7,15},{8,0},{9,1},... | collective-permute-start | bytes 98312 | tf_op jit(solution)/shard_map/ppermute | solution.py:22
  228.7 22.6 %collective-permute-start.8 = (f32[4,16,128]{2,1,0:T(8,128)S(1)}, f32[4,16,128]{2,1,0:T(8,128)S(1)}, u32[]{:S(2)}, u32[]{:S(2)}) collective-permute-start(f32[4,16,128]{2,1,0:T(8,128)S(1)} %bitcast.379), channel_id=1, source_target_pairs={{0,9},{1,8},{2,11},{3,10},{4,13},{5,12},{6,15},{7,14},{8,1},{9,0},... | collective-permute-start | bytes 98312 | tf_op jit(solution)/shard_map/ppermute | solution.py:22
  234.9 18.3 %collective-permute-start.9 = (f32[4,16,128]{2,1,0:T(8,128)S(1)}, f32[4,16,128]{2,1,0:T(8,128)S(1)}, u32[]{:S(2)}, u32[]{:S(2)}) collective-permute-start(f32[4,16,128]{2,1,0:T(8,128)S(1)} %bitcast.378), channel_id=1, source_target_pairs={{0,10},{1,11},{2,8},{3,9},{4,14},{5,15},{6,12},{7,13},{8,2},{9,3},... | collective-permute-start | bytes 98312 | tf_op jit(solution)/shard_map/ppermute | solution.py:22
  236.8 21.7 %collective-permute-start.10 = (f32[4,16,128]{2,1,0:T(8,128)S(1)}, f32[4,16,128]{2,1,0:T(8,128)S(1)}, u32[]{:S(2)}, u32[]{:S(2)}) collective-permute-start(f32[4,16,128]{2,1,0:T(8,128)S(1)} %bitcast.377), channel_id=1, source_target_pairs={{0,11},{1,10},{2,9},{3,8},{4,15},{5,14},{6,13},{7,12},{8,3},{9,2},... | collective-permute-start | bytes 98312 | tf_op jit(solution)/shard_map/ppermute | solution.py:22
  243.9 14.6 %collective-permute-start.11 = (f32[4,16,128]{2,1,0:T(8,128)S(1)}, f32[4,16,128]{2,1,0:T(8,128)S(1)}, u32[]{:S(2)}, u32[]{:S(2)}) collective-permute-start(f32[4,16,128]{2,1,0:T(8,128)S(1)} %bitcast.376), channel_id=1, source_target_pairs={{0,12},{1,13},{2,14},{3,15},{4,8},{5,9},{6,10},{7,11},{8,4},{9,5},... | collective-permute-start | bytes 98312 | tf_op jit(solution)/shard_map/ppermute | solution.py:22
  245.9 12.7 %collective-permute-start.12 = (f32[4,16,128]{2,1,0:T(8,128)S(1)}, f32[4,16,128]{2,1,0:T(8,128)S(1)}, u32[]{:S(2)}, u32[]{:S(2)}) collective-permute-start(f32[4,16,128]{2,1,0:T(8,128)S(1)} %bitcast.375), channel_id=1, source_target_pairs={{0,13},{1,12},{2,15},{3,14},{4,9},{5,8},{6,11},{7,10},{8,5},{9,4},... | collective-permute-start | bytes 98312 | tf_op jit(solution)/shard_map/ppermute | solution.py:22
  251.3 7.3 %collective-permute-start.13 = (f32[4,16,128]{2,1,0:T(8,128)S(1)}, f32[4,16,128]{2,1,0:T(8,128)S(1)}, u32[]{:S(2)}, u32[]{:S(2)}) collective-permute-start(f32[4,16,128]{2,1,0:T(8,128)S(1)} %bitcast.374), channel_id=1, source_target_pairs={{0,14},{1,15},{2,12},{3,13},{4,10},{5,11},{6,8},{7,9},{8,6},{9,7},... | collective-permute-start | bytes 98312 | tf_op jit(solution)/shard_map/ppermute | solution.py:22
  253.2 6.8 %collective-permute-start.14 = (f32[4,16,128]{2,1,0:T(8,128)S(1)}, f32[4,16,128]{2,1,0:T(8,128)S(1)}, u32[]{:S(2)}, u32[]{:S(2)}) collective-permute-start(f32[4,16,128]{2,1,0:T(8,128)S(1)} %bitcast.373), channel_id=1, source_target_pairs={{0,15},{1,14},{2,13},{3,12},{4,11},{5,10},{6,9},{7,8},{8,7},{9,6},... | collective-permute-start | bytes 98312 | tf_op jit(solution)/shard_map/ppermute | solution.py:22
